TPU v7x, 128 devices: a whole 4x4x4 slice. The times are simulated.
128 devices in a mesh: prow: 8 (over y, core), pcol: 16 (over x, z).
Axes of the slice: x: 4, y: 4, z: 4, core: 2. Of those that a mesh axis runs over, the one named last changes fastest.
Arguments:
- right_sides: bfloat16 [32768, 128], P(('prow', 'pcol')), may hold values from -6 to 6
- factor: bfloat16 [16, 16, 32, 8, 128, 128], P(None, 'pcol', None, 'prow'), may hold values from -0.046875 to 0.046875
- pattern: int32 [16, 16, 32, 8], P(None, 'pcol', None, 'prow'), may hold values 0 or 1
- lower_inverse: bfloat16 [16, 16, 128, 128], P(None, 'pcol'), may hold values from -0.5 to 0.5
- upper_inverse: bfloat16 [16, 16, 128, 128], P(None, 'pcol'), may hold values from -0.5 to 0.5
Outputs:
- solution: bfloat16 [32768, 128], P(('prow', 'pcol'))
All inputs are finite; a program needn't handle non-finite values. No bound on the sum of `pattern` on one device may be relied on, other than what follows from the above.
Results may differ from a plain program's by a relative error of at most 0.02.
Values may be sent and summed in bfloat16 or wider, within the bound.
A program may use at most 128 MiB of HBM per device.

v0:
```python
import jax
import jax.numpy as jnp
from jax import lax
from jax.sharding import PartitionSpec as P


def level_index(index_vals, node_count):
    bounds = (node_count // 2, 3 * node_count // 4, 7 * node_count // 8)
    result = jnp.zeros(index_vals.shape, jnp.int32)
    for edge_val in bounds:
        result = result + (index_vals >= edge_val).astype(jnp.int32)
    return result


def level_sums(
    blocks,
    pattern_loc,
    col_levels,
    solved_all,
    row_id,
    prow_n,
    row_start,
    row_end,
    col_start,
    col_end,
    level_id,
    upward,
):
    if col_end <= col_start:
        return None
    block_size = blocks.shape[2]
    rhs_count = solved_all.shape[2]
    grouped = solved_all.reshape(-1, prow_n, block_size, rhs_count)
    column_vals = lax.dynamic_index_in_dim(grouped, row_id, 1, keepdims=False)[col_start:col_end]
    levels_here = col_levels[col_start:col_end]
    if upward:
        order_mask = levels_here > level_id
    else:
        order_mask = levels_here < level_id
    keep_mask = (pattern_loc[row_start:row_end, col_start:col_end] > 0) & order_mask[None, :]
    masked = jnp.where(
        keep_mask[:, :, None, None],
        blocks[row_start:row_end, col_start:col_end],
        jnp.zeros((), jnp.bfloat16),
    )
    return jnp.einsum("ijab,jbn->ian", masked, column_vals, preferred_element_type=jnp.float32)


def finish_level(partial_value, base_rows, inverse_rows, pcol_n):
    row_count = base_rows.shape[0]
    block_size = base_rows.shape[1]
    rhs_count = base_rows.shape[2]
    if partial_value is None:
        remainder = base_rows
    else:
        summed = lax.psum(partial_value.astype(jnp.bfloat16), "prow").astype(jnp.float32)
        remainder = (base_rows.astype(jnp.float32) - summed).astype(jnp.bfloat16)
    solved = jnp.einsum(
        "iab,ibn->ian", inverse_rows, remainder, preferred_element_type=jnp.float32
    ).astype(jnp.bfloat16)
    gathered = lax.all_gather(solved[:, None], "pcol", axis=1, tiled=True)
    return gathered.reshape(row_count * pcol_n, block_size, rhs_count)


def on_device(right_sides, factor, pattern, lower_inverse, upper_inverse):
    prow_n = lax.axis_size("prow")
    pcol_n = lax.axis_size("pcol")
    row_id = lax.axis_index("prow")
    col_id = lax.axis_index("pcol")
    blocks = factor[:, 0, :, 0]
    pattern_loc = pattern[:, 0, :, 0]
    lower_rows = lower_inverse[:, 0]
    upper_rows = upper_inverse[:, 0]
    row_blocks = blocks.shape[0]
    col_blocks = blocks.shape[1]
    block_size = blocks.shape[2]
    rhs_count = right_sides.shape[1]
    node_count = row_blocks * pcol_n
    everything = lax.all_gather(right_sides, ("prow", "pcol"), axis=0, tiled=True)
    everything = everything.reshape(row_blocks, pcol_n, block_size, rhs_count)
    mine_right = lax.dynamic_index_in_dim(everything, col_id, 1, keepdims=False)
    col_levels = level_index(jnp.arange(col_blocks, dtype=jnp.int32) * prow_n + row_id, node_count)
    bounds = (0, row_blocks // 2, 3 * row_blocks // 4, 7 * row_blocks // 8, row_blocks)
    forward_vals = jnp.zeros((node_count, block_size, rhs_count), jnp.bfloat16)
    for level_id in range(4):
        row_start, row_end = (bounds[level_id], bounds[level_id + 1])
        col_end = min(col_blocks, -(-(row_start * pcol_n) // prow_n))
        partial_value = level_sums(
            blocks,
            pattern_loc,
            col_levels,
            forward_vals,
            row_id,
            prow_n,
            row_start,
            row_end,
            0,
            col_end,
            level_id,
            False,
        )
        solved = finish_level(
            partial_value, mine_right[row_start:row_end], lower_rows[row_start:row_end], pcol_n
        )
        forward_vals = lax.dynamic_update_slice_in_dim(forward_vals, solved, row_start * pcol_n, 0)
    forward_mine = lax.dynamic_index_in_dim(
        forward_vals.reshape(row_blocks, pcol_n, block_size, rhs_count), col_id, 1, keepdims=False
    )
    backward_vals = jnp.zeros((node_count, block_size, rhs_count), jnp.bfloat16)
    for level_id in (3, 2, 1, 0):
        row_start, row_end = (bounds[level_id], bounds[level_id + 1])
        col_start = row_end * pcol_n // prow_n
        partial_value = level_sums(
            blocks,
            pattern_loc,
            col_levels,
            backward_vals,
            row_id,
            prow_n,
            row_start,
            row_end,
            col_start,
            col_blocks,
            level_id,
            True,
        )
        solved = finish_level(
            partial_value, forward_mine[row_start:row_end], upper_rows[row_start:row_end], pcol_n
        )
        backward_vals = lax.dynamic_update_slice_in_dim(
            backward_vals, solved, row_start * pcol_n, 0
        )
    out_rows = right_sides.shape[0]
    device_id = row_id * pcol_n + col_id
    flat = backward_vals.reshape(node_count * block_size, rhs_count)
    return lax.dynamic_slice_in_dim(flat, device_id * out_rows, out_rows, 0)


def solution(mesh):
    placed = (
        P(("prow", "pcol"), None),
        P(None, "pcol", None, "prow", None, None),
        P(None, "pcol", None, "prow"),
        P(None, "pcol", None, None),
        P(None, "pcol", None, None),
    )
    return jax.shard_map(
        on_device, mesh=mesh, in_specs=placed, out_specs=P(("prow", "pcol"), None), check_vma=False
    )
```

profile of v0, /device:TPU:0, one launch (start us, length us, event | category | flops | bytes accessed | tf_op | source)
XLA Modules:
  0.0 902.8 jit_solution(18157509265006647587)
XLA Ops:
  7.3 75.4 %all-gather.18.cloned.1.call-done = bf16[32768,128]{1,0:T(8,128)(2,1)} async-done(((bf16[256,128]{1,0:T(8,128)(2,1)}), bf16[32768,128]{1,0:T(8,128)(2,1)}) %all-gather.18.cloned.1.call-update) | async-done | bytes 8388624 | tf_op jit(solution)/shard_map/all_gather | solution.py:79
  82.7 2.1 fusion.11
  85.7 53.7 %all-gather.20.cloned.1.call-done = bf16[8,2048,128]{1,2,0:T(8,128)(2,1)} async-done(((bf16[8,128,128]{1,2,0:T(8,128)(2,1)}), bf16[8,2048,128]{1,2,0:T(8,128)(2,1)}) %all-gather.20.cloned.1.call-update) | async-done | bytes 4194320 | tf_op jit(solution)/shard_map/all_gather | solution.py:61
  139.4 6.5 copy.16
  145.9 4.1 dynamic_update_slice.24
  150.0 3.2 copy-done
  153.2 3.1 fusion.15
  157.5 58.3 %all-reduce.9.cloned.1.call-done = bf16[4,128,128]{1,2,0:T(8,128)(2,1)} async-done(((bf16[4,128,128]{1,2,0:T(8,128)(2,1)}), bf16[4,128,128]{1,2,0:T(8,128)(2,1)}) %all-reduce.9.cloned.1.call-update) | async-done | bytes 131088 | tf_op jit(solution)/shard_map/psum | solution.py:56
  215.8 1.8 fusion.17
  217.7 46.2 %all-gather.22.cloned.1.call-done = bf16[4,2048,128]{1,2,0:T(8,128)(2,1)} async-done(((bf16[4,128,128]{1,2,0:T(8,128)(2,1)}), bf16[4,2048,128]{1,2,0:T(8,128)(2,1)}) %all-gather.22.cloned.1.call-update) | async-done | bytes 2097168 | tf_op jit(solution)/shard_map/all_gather | solution.py:61
  263.9 3.0 copy.18
  267.0 1.4 constant_dynamic-update-slice_fusion.5
  268.4 3.0 fusion.22
  272.6 58.2 %all-reduce.11.cloned.1.call-done = bf16[2,128,128]{1,2,0:T(8,128)(2,1)} async-done(((bf16[2,128,128]{1,2,0:T(8,128)(2,1)}), bf16[2,128,128]{1,2,0:T(8,128)(2,1)}) %all-reduce.11.cloned.1.call-update) | async-done | bytes 65552 | tf_op jit(solution)/shard_map/psum | solution.py:56
  330.8 1.6 fusion.23
  332.5 42.4 %all-gather.24.cloned.1.call-done = bf16[2,2048,128]{1,2,0:T(8,128)(2,1)} async-done(((bf16[2,128,128]{1,2,0:T(8,128)(2,1)}), bf16[2,2048,128]{1,2,0:T(8,128)(2,1)}) %all-gather.24.cloned.1.call-update) | async-done | bytes 1048592 | tf_op jit(solution)/shard_map/all_gather | solution.py:61
  374.9 1.6 copy.20
  376.5 1.1 constant_dynamic-update-slice_fusion.4
  377.6 3.2 fusion.20
  381.0 59.0 %all-reduce.13.cloned.1.call-done = bf16[2,128,128]{1,2,0:T(8,128)(2,1)} async-done(((bf16[2,128,128]{1,2,0:T(8,128)(2,1)}), bf16[2,128,128]{1,2,0:T(8,128)(2,1)}) %all-reduce.13.cloned.1.call-update) | async-done | bytes 65552 | tf_op jit(solution)/shard_map/psum | solution.py:56
  440.0 1.6 fusion.24
  441.7 42.6 %all-gather.26.cloned.1.call-done = bf16[2,2048,128]{1,2,0:T(8,128)(2,1)} async-done(((bf16[2,128,128]{1,2,0:T(8,128)(2,1)}), bf16[2,2048,128]{1,2,0:T(8,128)(2,1)}) %all-gather.26.cloned.1.call-update) | async-done | bytes 1048592 | tf_op jit(solution)/shard_map/all_gather | solution.py:61
  484.3 1.6 copy.22
  485.9 1.1 constant_dynamic-update-slice_fusion.3
  487.0 1.7 fusion.25
  488.9 42.5 %all-gather.28.cloned.1.call-done = bf16[2,2048,128]{1,2,0:T(8,128)(2,1)} async-done(((bf16[2,128,128]{1,2,0:T(8,128)(2,1)}), bf16[2,2048,128]{1,2,0:T(8,128)(2,1)}) %all-gather.28.cloned.1.call-update) | async-done | bytes 1048592 | tf_op jit(solution)/shard_map/all_gather | solution.py:61
  531.3 1.6 copy.25
  533.0 5.3 dynamic_update_slice.28
  538.3 1.9 fusion.21
  541.3 58.2 %all-reduce.15.cloned.1.call-done = bf16[2,128,128]{1,2,0:T(8,128)(2,1)} async-done(((bf16[2,128,128]{1,2,0:T(8,128)(2,1)}), bf16[2,128,128]{1,2,0:T(8,128)(2,1)}) %all-reduce.15.cloned.1.call-update) | async-done | bytes 65552 | tf_op jit(solution)/shard_map/psum | solution.py:56
  599.4 1.6 fusion.26
  601.3 42.4 %all-gather.30.cloned.1.call-done = bf16[2,2048,128]{1,2,0:T(8,128)(2,1)} async-done(((bf16[2,128,128]{1,2,0:T(8,128)(2,1)}), bf16[2,2048,128]{1,2,0:T(8,128)(2,1)}) %all-gather.30.cloned.1.call-update) | async-done | bytes 1048592 | tf_op jit(solution)/shard_map/all_gather | solution.py:61
  643.7 1.6 copy.27
  645.3 1.0 constant_dynamic-update-slice_fusion.2
  646.4 2.5 fusion.14
  650.0 58.2 %all-reduce.17.cloned.1.call-done = bf16[4,128,128]{1,2,0:T(8,128)(2,1)} async-done(((bf16[4,128,128]{1,2,0:T(8,128)(2,1)}), bf16[4,128,128]{1,2,0:T(8,128)(2,1)}) %all-reduce.17.cloned.1.call-update) | async-done | bytes 131088 | tf_op jit(solution)/shard_map/psum | solution.py:56
  708.2 1.8 fusion.18
  710.1 46.3 %all-gather.32.cloned.1.call-done = bf16[4,2048,128]{1,2,0:T(8,128)(2,1)} async-done(((bf16[4,128,128]{1,2,0:T(8,128)(2,1)}), bf16[4,2048,128]{1,2,0:T(8,128)(2,1)}) %all-gather.32.cloned.1.call-update) | async-done | bytes 2097168 | tf_op jit(solution)/shard_map/all_gather | solution.py:61
  756.5 3.0 copy.29
  759.5 1.5 constant_dynamic-update-slice_fusion.1
  761.0 4.6 fusion.10
  765.6 1.0 constant_dynamic-slice_fusion.5
  766.8 58.6 %all-reduce.19.cloned.1.call-done = bf16[8,128,128]{1,2,0:T(8,128)(2,1)} async-done(((bf16[8,128,128]{1,2,0:T(8,128)(2,1)}), bf16[8,128,128]{1,2,0:T(8,128)(2,1)}) %all-reduce.19.cloned.1.call-update) | async-done | bytes 262160 | tf_op jit(solution)/shard_map/psum | solution.py:56
  825.4 2.0 fusion.12
  827.4 56.1 %all-gather.34.cloned.1.call-done = bf16[8,2048,128]{1,2,0:T(8,128)(2,1)} async-done(((bf16[8,128,128]{1,2,0:T(8,128)(2,1)}), bf16[8,2048,128]{1,2,0:T(8,128)(2,1)}) %all-gather.34.cloned.1.call-update) | async-done | bytes 4194320 | tf_op jit(solution)/shard_map/all_gather | solution.py:61
  883.5 6.5 copy.31
  890.0 4.7 constant_dynamic-update-slice_fusion
  894.8 1.5 constant_dynamic-slice_fusion.4
  (59 shorter events, 7.1 us)
Async XLA Ops:
  6.5 76.2 %all-gather.18.cloned.1.call-start = ((), (), s32[]{:S(2)}) async-start(), calls=%async_computation | async-start | bytes 8454144 | tf_op jit(solution)/shard_map/all_gather | solution.py:79
  7.3 132.1 %all-gather.20.cloned.1.call-start = ((), (), s32[]{:S(2)}) async-start(), calls=%async_computation.7 | async-start | bytes 4456448 | tf_op jit(solution)/shard_map/all_gather | solution.py:61
  84.8 131.0 %all-reduce.9.cloned.1.call-start = ((), (), s32[]{:S(2)}) async-start(), calls=%async_computation.1 | async-start | bytes 262144 | tf_op jit(solution)/shard_map/psum | solution.py:56
  145.9 69.9 %copy-start.1 = (bf16[16,1,128,128]{3,2,1,0:T(8,128)(2,1)S(1)}, bf16[16,1,128,128]{3,2,1,0:T(8,128)(2,1)}, u32[]{:S(2)}) copy-start(bf16[16,1,128,128]{3,2,1,0:T(8,128)(2,1)} %param.8) | copy-start | bytes 1572868
  145.9 71.8 %copy-start.3 = (s32[16,1,32,1]{2,3,1,0:T(1,128)S(1)}, s32[16,1,32,1]{2,3,1,0:T(1,128)}, u32[]{:S(2)}) copy-start(s32[16,1,32,1]{2,3,1,0:T(1,128)} %param.7) | copy-start | bytes 6148
  150.0 3.2 copy-start
  156.4 107.5 %all-gather.22.cloned.1.call-start = ((), (), s32[]{:S(2)}) async-start(), calls=%async_computation.8 | async-start | bytes 2228224 | tf_op jit(solution)/shard_map/all_gather | solution.py:61
  217.6 113.2 %all-reduce.11.cloned.1.call-start = ((), (), s32[]{:S(2)}) async-start(), calls=%async_computation.2 | async-start | bytes 131072 | tf_op jit(solution)/shard_map/psum | solution.py:56
  268.4 218.5 %copy-start.2 = (bf16[16,1,128,128]{3,2,1,0:T(8,128)(2,1)S(1)}, bf16[16,1,128,128]{3,2,1,0:T(8,128)(2,1)}, u32[]{:S(2)}) copy-start(bf16[16,1,128,128]{3,2,1,0:T(8,128)(2,1)} %param.9) | copy-start | bytes 1572868
  271.5 103.4 %all-gather.24.cloned.1.call-start = ((), (), s32[]{:S(2)}) async-start(), calls=%async_computation.9 | async-start | bytes 1114112 | tf_op jit(solution)/shard_map/all_gather | solution.py:61
  332.4 107.6 %all-reduce.13.cloned.1.call-start = ((), (), s32[]{:S(2)}) async-start(), calls=%async_computation.3 | async-start | bytes 131072 | tf_op jit(solution)/shard_map/psum | solution.py:56
  380.8 103.5 %all-gather.26.cloned.1.call-start = ((), (), s32[]{:S(2)}) async-start(), calls=%async_computation.10 | async-start | bytes 1114112 | tf_op jit(solution)/shard_map/all_gather | solution.py:61
  441.7 89.7 %all-gather.28.cloned.1.call-start = ((), (), s32[]{:S(2)}) async-start(), calls=%async_computation.11 | async-start | bytes 1114112 | tf_op jit(solution)/shard_map/all_gather | solution.py:61
  488.7 110.8 %all-reduce.15.cloned.1.call-start = ((), (), s32[]{:S(2)}) async-start(), calls=%async_computation.4 | async-start | bytes 131072 | tf_op jit(solution)/shard_map/psum | solution.py:56
  540.2 103.5 %all-gather.30.cloned.1.call-start = ((), (), s32[]{:S(2)}) async-start(), calls=%async_computation.12 | async-start | bytes 1114112 | tf_op jit(solution)/shard_map/all_gather | solution.py:61
  601.1 107.1 %all-reduce.17.cloned.1.call-start = ((), (), s32[]{:S(2)}) async-start(), calls=%async_computation.5 | async-start | bytes 262144 | tf_op jit(solution)/shard_map/psum | solution.py:56
  648.9 107.6 %all-gather.32.cloned.1.call-start = ((), (), s32[]{:S(2)}) async-start(), calls=%async_computation.13 | async-start | bytes 2228224 | tf_op jit(solution)/shard_map/all_gather | solution.py:61
  710.0 115.4 %all-reduce.19.cloned.1.call-start = ((), (), s32[]{:S(2)}) async-start(), calls=%async_computation.6 | async-start | bytes 524288 | tf_op jit(solution)/shard_map/psum | solution.py:56
  765.6 117.9 %all-gather.34.cloned.1.call-start = ((), (), s32[]{:S(2)}) async-start(), calls=%async_computation.14 | async-start | bytes 4456448 | tf_op jit(solution)/shard_map/all_gather | solution.py:61
Sparse Core Ops, SparseCore 0:
  10.5 72.1 all-gather.17
  84.9 54.4 all-gather.19
  156.5 59.2 all-reduce.8
  217.8 46.0 all-gather.21
  271.6 59.1 all-reduce.10
  332.7 42.1 all-gather.23
  380.9 59.0 all-reduce.12
  442.1 42.1 all-gather.25
  488.8 42.5 all-gather.27
  540.4 59.0 all-reduce.14
  601.6 42.1 all-gather.29
  649.0 59.1 all-reduce.16
  710.3 46.0 all-gather.31
  765.7 59.6 all-reduce.18
  827.5 55.9 all-gather.33
where the time goes:
time: 904 us; the launch traced here: 903 us
  waiting for transfers between devices  799 us (88%)
  local copies, waits for them, and re-layouts  55.9 us (6%)
  matrix products  32.5 us (4%)
  between operations  13.5 us (1%)
    all_gather x8, waiting for transfers between devices, finish_level(): gathered = lax.all_gather(solved[:, None], 'pcol', axis=1, tiled=True)  372 us
    psum x6, waiting for transfers between devices, finish_level(): lax.psum(partial_value.astype(jnp.bfloat16), 'prow').astype(jnp.float32)  351 us
    all_gather x1, waiting for transfers between devices, on_device(): lax.all_gather(right_sides, ('prow', 'pcol'), axis=0, tiled=True)  75.4 us
    all_gather x8, local copies, waits for them, and re-layouts, finish_level(): gathered = lax.all_gather(solved[:, None], 'pcol', axis=1, tiled=True)  25.4 us
    dot_general x6, matrix products, level_sums(): jnp.einsum('ijab,jbn->ian', masked, column_vals, preferred_element_type=j...  18.3 us
  transfers between devices with their start and end apart: 15, of which 15 were waited for; matrix products, arithmetic and copies ran while one was open for 1% of the time, Pallas kernels for 0%

commit v1 on v0

--- a/solution.py
+++ b/solution.py
@@ -76,7 +76,12 @@
     block_size = blocks.shape[2]
     rhs_count = right_sides.shape[1]
     node_count = row_blocks * pcol_n
-    everything = lax.all_gather(right_sides, ("prow", "pcol"), axis=0, tiled=True)
+    everything = jnp.concatenate(
+        lax.all_to_all(
+            jnp.stack([right_sides] * lax.axis_size(("prow", "pcol"))), ("prow", "pcol"), 0, 0
+        ),
+        axis=0,
+    )
     everything = everything.reshape(row_blocks, pcol_n, block_size, rhs_count)
     mine_right = lax.dynamic_index_in_dim(everything, col_id, 1, keepdims=False)
     col_levels = level_index(jnp.arange(col_blocks, dtype=jnp.int32) * prow_n + row_id, node_count)

time: 904 us -> 948 us (1.049)
  waiting for transfers between devices: 799 us -> 826 us
  starting transfers between devices: 0.58 us -> 12.5 us
    all_to_all x0 -> x1, waiting for transfers between devices: none -> 99.9 us  [on_device(): lax.all_to_all(jnp.stack([right_sides] * lax.axis_size(('prow', 'pcol')))...]
    all_gather x1 -> x0, waiting for transfers between devices: 75.4 us -> none  [on_device(): lax.all_gather(right_sides, ('prow', 'pcol'), axis=0, tiled=True)]
    all_to_all x0 -> x1, starting transfers between devices: none -> 11.7 us  [on_device(): lax.all_to_all(jnp.stack([right_sides] * lax.axis_size(('prow', 'pcol')))...]
where the time goes in v1:
time: 948 us; the launch traced here: 947 us
  waiting for transfers between devices  826 us (87%)
  local copies, waits for them, and re-layouts  62 us (7%)
  matrix products  32.4 us (3%)
  between operations  13.5 us (1%)
  starting transfers between devices  12.5 us (1%)
    all_gather x8, waiting for transfers between devices, finish_level(): gathered = lax.all_gather(solved[:, None], 'pcol', axis=1, tiled=True)  376 us
    psum x6, waiting for transfers between devices, finish_level(): lax.psum(partial_value.astype(jnp.bfloat16), 'prow').astype(jnp.float32)  351 us
    all_to_all x1, waiting for transfers between devices, on_device(): lax.all_to_all(jnp.stack([right_sides] * lax.axis_size(('prow', 'pcol')))...  99.9 us
    all_gather x8, local copies, waits for them, and re-layouts, finish_level(): gathered = lax.all_gather(solved[:, None], 'pcol', axis=1, tiled=True)  25.5 us
  transfers between devices with their start and end apart: 15, of which 15 were waited for; matrix products, arithmetic and copies ran while one was open for 1% of the time, Pallas kernels for 0%

profile of v1, /device:TPU:0, one launch (start us, length us, event | category | flops | bytes accessed | tf_op | source)
XLA Modules:
  0.0 947.0 jit_solution(15998056923002841139)
XLA Ops:
  6.5 6.2 stack.2
  12.7 11.7 %all-to-all-start = ((bf16[128,256,128]{2,1,0:T(8,128)(2,1)}), bf16[128,256,128]{2,1,0:T(8,128)(2,1)}, u32[]{:S(2)}, u32[]{:S(2)}) async-start(bf16[128,256,128]{2,1,0:T(8,128)(2,1)} %stack.2), calls=%async_computation | async-start | bytes 16777216 | tf_op jit(solution)/shard_map/all_to_all | solution.py:80
  24.5 99.9 %all-to-all-done = bf16[128,256,128]{2,1,0:T(8,128)(2,1)} async-done(((bf16[128,256,128]{2,1,0:T(8,128)(2,1)}), bf16[128,256,128]{2,1,0:T(8,128)(2,1)}, u32[]{:S(2)}, u32[]{:S(2)}) %all-to-all-start) | async-done | bytes 8388640 | tf_op jit(solution)/shard_map/all_to_all | solution.py:80
  124.3 2.0 fusion.11
  126.5 57.3 %all-gather.17.cloned.1.call-done = bf16[8,2048,128]{1,2,0:T(8,128)(2,1)} async-done(((bf16[8,128,128]{1,2,0:T(8,128)(2,1)}), bf16[8,2048,128]{1,2,0:T(8,128)(2,1)}) %all-gather.17.cloned.1.call-update) | async-done | bytes 4194320 | tf_op jit(solution)/shard_map/all_gather | solution.py:61
  183.8 6.5 copy.16
  190.3 4.1 dynamic_update_slice.24
  194.3 3.2 copy-done
  197.6 3.1 fusion.15
  201.8 58.3 %all-reduce.9.cloned.1.call-done = bf16[4,128,128]{1,2,0:T(8,128)(2,1)} async-done(((bf16[4,128,128]{1,2,0:T(8,128)(2,1)}), bf16[4,128,128]{1,2,0:T(8,128)(2,1)}) %all-reduce.9.cloned.1.call-update) | async-done | bytes 131088 | tf_op jit(solution)/shard_map/psum | solution.py:56
  260.1 1.8 fusion.17
  262.0 46.4 %all-gather.19.cloned.1.call-done = bf16[4,2048,128]{1,2,0:T(8,128)(2,1)} async-done(((bf16[4,128,128]{1,2,0:T(8,128)(2,1)}), bf16[4,2048,128]{1,2,0:T(8,128)(2,1)}) %all-gather.19.cloned.1.call-update) | async-done | bytes 2097168 | tf_op jit(solution)/shard_map/all_gather | solution.py:61
  308.4 3.0 copy.18
  311.4 1.4 constant_dynamic-update-slice_fusion.5
  312.9 3.0 fusion.22
  317.0 58.2 %all-reduce.11.cloned.1.call-done = bf16[2,128,128]{1,2,0:T(8,128)(2,1)} async-done(((bf16[2,128,128]{1,2,0:T(8,128)(2,1)}), bf16[2,128,128]{1,2,0:T(8,128)(2,1)}) %all-reduce.11.cloned.1.call-update) | async-done | bytes 65552 | tf_op jit(solution)/shard_map/psum | solution.py:56
  375.2 1.6 fusion.23
  377.0 42.4 %all-gather.21.cloned.1.call-done = bf16[2,2048,128]{1,2,0:T(8,128)(2,1)} async-done(((bf16[2,128,128]{1,2,0:T(8,128)(2,1)}), bf16[2,2048,128]{1,2,0:T(8,128)(2,1)}) %all-gather.21.cloned.1.call-update) | async-done | bytes 1048592 | tf_op jit(solution)/shard_map/all_gather | solution.py:61
  419.4 1.6 copy.20
  421.0 1.1 constant_dynamic-update-slice_fusion.4
  422.1 3.2 fusion.20
  425.5 59.0 %all-reduce.13.cloned.1.call-done = bf16[2,128,128]{1,2,0:T(8,128)(2,1)} async-done(((bf16[2,128,128]{1,2,0:T(8,128)(2,1)}), bf16[2,128,128]{1,2,0:T(8,128)(2,1)}) %all-reduce.13.cloned.1.call-update) | async-done | bytes 65552 | tf_op jit(solution)/shard_map/psum | solution.py:56
  484.5 1.6 fusion.24
  486.2 42.6 %all-gather.23.cloned.1.call-done = bf16[2,2048,128]{1,2,0:T(8,128)(2,1)} async-done(((bf16[2,128,128]{1,2,0:T(8,128)(2,1)}), bf16[2,2048,128]{1,2,0:T(8,128)(2,1)}) %all-gather.23.cloned.1.call-update) | async-done | bytes 1048592 | tf_op jit(solution)/shard_map/all_gather | solution.py:61
  528.8 1.6 copy.22
  530.4 1.1 constant_dynamic-update-slice_fusion.3
  531.4 1.7 fusion.25
  533.4 42.5 %all-gather.25.cloned.1.call-done = bf16[2,2048,128]{1,2,0:T(8,128)(2,1)} async-done(((bf16[2,128,128]{1,2,0:T(8,128)(2,1)}), bf16[2,2048,128]{1,2,0:T(8,128)(2,1)}) %all-gather.25.cloned.1.call-update) | async-done | bytes 1048592 | tf_op jit(solution)/shard_map/all_gather | solution.py:61
  575.8 1.6 copy.25
  577.4 5.3 dynamic_update_slice.28
  582.8 1.9 fusion.21
  585.7 58.2 %all-reduce.15.cloned.1.call-done = bf16[2,128,128]{1,2,0:T(8,128)(2,1)} async-done(((bf16[2,128,128]{1,2,0:T(8,128)(2,1)}), bf16[2,128,128]{1,2,0:T(8,128)(2,1)}) %all-reduce.15.cloned.1.call-update) | async-done | bytes 65552 | tf_op jit(solution)/shard_map/psum | solution.py:56
  643.9 1.6 fusion.26
  645.8 42.3 %all-gather.27.cloned.1.call-done = bf16[2,2048,128]{1,2,0:T(8,128)(2,1)} async-done(((bf16[2,128,128]{1,2,0:T(8,128)(2,1)}), bf16[2,2048,128]{1,2,0:T(8,128)(2,1)}) %all-gather.27.cloned.1.call-update) | async-done | bytes 1048592 | tf_op jit(solution)/shard_map/all_gather | solution.py:61
  688.0 1.6 copy.27
  690.7 2.5 fusion.14
  694.3 58.2 %all-reduce.17.cloned.1.call-done = bf16[4,128,128]{1,2,0:T(8,128)(2,1)} async-done(((bf16[4,128,128]{1,2,0:T(8,128)(2,1)}), bf16[4,128,128]{1,2,0:T(8,128)(2,1)}) %all-reduce.17.cloned.1.call-update) | async-done | bytes 131088 | tf_op jit(solution)/shard_map/psum | solution.py:56
  752.5 1.8 fusion.18
  754.6 46.0 %all-gather.29.cloned.1.call-done = bf16[4,2048,128]{1,2,0:T(8,128)(2,1)} async-done(((bf16[4,128,128]{1,2,0:T(8,128)(2,1)}), bf16[4,2048,128]{1,2,0:T(8,128)(2,1)}) %all-gather.29.cloned.1.call-update) | async-done | bytes 2097168 | tf_op jit(solution)/shard_map/all_gather | solution.py:61
  800.6 3.0 copy.29
  803.7 1.5 constant_dynamic-update-slice_fusion.1
  805.2 4.6 fusion.10
  811.0 58.6 %all-reduce.19.cloned.1.call-done = bf16[8,128,128]{1,2,0:T(8,128)(2,1)} async-done(((bf16[8,128,128]{1,2,0:T(8,128)(2,1)}), bf16[8,128,128]{1,2,0:T(8,128)(2,1)}) %all-reduce.19.cloned.1.call-update) | async-done | bytes 262160 | tf_op jit(solution)/shard_map/psum | solution.py:56
  869.6 2.0 fusion.12
  871.6 56.1 %all-gather.31.cloned.1.call-done = bf16[8,2048,128]{1,2,0:T(8,128)(2,1)} async-done(((bf16[8,128,128]{1,2,0:T(8,128)(2,1)}), bf16[8,2048,128]{1,2,0:T(8,128)(2,1)}) %all-gather.31.cloned.1.call-update) | async-done | bytes 4194320 | tf_op jit(solution)/shard_map/all_gather | solution.py:61
  927.7 6.5 copy.31
  934.2 4.7 constant_dynamic-update-slice_fusion
  939.0 1.5 constant_dynamic-slice_fusion.4
  (59 shorter events, 7.9 us)
Async XLA Ops:
  12.7 111.6 %copy-start.1 = (bf16[16,1,128,128]{3,2,1,0:T(8,128)(2,1)S(1)}, bf16[16,1,128,128]{3,2,1,0:T(8,128)(2,1)}, u32[]{:S(2)}) copy-start(bf16[16,1,128,128]{3,2,1,0:T(8,128)(2,1)} %param.8) | copy-start | bytes 1572868
  12.7 113.8 %copy-start.3 = (s32[16,1,32,1]{2,3,1,0:T(1,128)S(1)}, s32[16,1,32,1]{2,3,1,0:T(1,128)}, u32[]{:S(2)}) copy-start(s32[16,1,32,1]{2,3,1,0:T(1,128)} %param.7) | copy-start | bytes 6148
  12.7 111.6 %all-to-all-start = ((bf16[128,256,128]{2,1,0:T(8,128)(2,1)}), bf16[128,256,128]{2,1,0:T(8,128)(2,1)}, u32[]{:S(2)}, u32[]{:S(2)}) async-start(bf16[128,256,128]{2,1,0:T(8,128)(2,1)} %stack.2), calls=%async_computation | async-start | bytes 16777216 | tf_op jit(solution)/shard_map/all_to_all | solution.py:80
  24.4 159.4 %all-gather.17.cloned.1.call-start = ((), (), s32[]{:S(2)}) async-start(), calls=%async_computation.7 | async-start | bytes 4456448 | tf_op jit(solution)/shard_map/all_gather | solution.py:61
  126.4 133.8 %all-reduce.9.cloned.1.call-start = ((), (), s32[]{:S(2)}) async-start(), calls=%async_computation.1 | async-start | bytes 262144 | tf_op jit(solution)/shard_map/psum | solution.py:56
  194.3 3.2 copy-start
  200.7 107.7 %all-gather.19.cloned.1.call-start = ((), (), s32[]{:S(2)}) async-start(), calls=%async_computation.8 | async-start | bytes 2228224 | tf_op jit(solution)/shard_map/all_gather | solution.py:61
  261.9 113.3 %all-reduce.11.cloned.1.call-start = ((), (), s32[]{:S(2)}) async-start(), calls=%async_computation.2 | async-start | bytes 131072 | tf_op jit(solution)/shard_map/psum | solution.py:56
  312.9 218.6 %copy-start.2 = (bf16[16,1,128,128]{3,2,1,0:T(8,128)(2,1)S(1)}, bf16[16,1,128,128]{3,2,1,0:T(8,128)(2,1)}, u32[]{:S(2)}) copy-start(bf16[16,1,128,128]{3,2,1,0:T(8,128)(2,1)} %param.9) | copy-start | bytes 1572868
  316.0 103.4 %all-gather.21.cloned.1.call-start = ((), (), s32[]{:S(2)}) async-start(), calls=%async_computation.9 | async-start | bytes 1114112 | tf_op jit(solution)/shard_map/all_gather | solution.py:61
  376.9 107.6 %all-reduce.13.cloned.1.call-start = ((), (), s32[]{:S(2)}) async-start(), calls=%async_computation.3 | async-start | bytes 131072 | tf_op jit(solution)/shard_map/psum | solution.py:56
  425.3 103.5 %all-gather.23.cloned.1.call-start = ((), (), s32[]{:S(2)}) async-start(), calls=%async_computation.10 | async-start | bytes 1114112 | tf_op jit(solution)/shard_map/all_gather | solution.py:61
  486.1 89.7 %all-gather.25.cloned.1.call-start = ((), (), s32[]{:S(2)}) async-start(), calls=%async_computation.11 | async-start | bytes 1114112 | tf_op jit(solution)/shard_map/all_gather | solution.py:61
  533.2 110.7 %all-reduce.15.cloned.1.call-start = ((), (), s32[]{:S(2)}) async-start(), calls=%async_computation.4 | async-start | bytes 131072 | tf_op jit(solution)/shard_map/psum | solution.py:56
  584.7 103.3 %all-gather.27.cloned.1.call-start = ((), (), s32[]{:S(2)}) async-start(), calls=%async_computation.12 | async-start | bytes 1114112 | tf_op jit(solution)/shard_map/all_gather | solution.py:61
  645.6 107.0 %all-reduce.17.cloned.1.call-start = ((), (), s32[]{:S(2)}) async-start(), calls=%async_computation.5 | async-start | bytes 262144 | tf_op jit(solution)/shard_map/psum | solution.py:56
  693.2 107.4 %all-gather.29.cloned.1.call-start = ((), (), s32[]{:S(2)}) async-start(), calls=%async_computation.13 | async-start | bytes 2228224 | tf_op jit(solution)/shard_map/all_gather | solution.py:61
  754.3 115.3 %all-reduce.19.cloned.1.call-start = ((), (), s32[]{:S(2)}) async-start(), calls=%async_computation.6 | async-start | bytes 524288 | tf_op jit(solution)/shard_map/psum | solution.py:56
  809.8 117.9 %all-gather.31.cloned.1.call-start = ((), (), s32[]{:S(2)}) async-start(), calls=%async_computation.14 | async-start | bytes 4456448 | tf_op jit(solution)/shard_map/all_gather | solution.py:61
Sparse Core Ops, SparseCore 0:
  126.5 57.2 all-gather.16
  200.8 59.2 all-reduce.8
  262.3 46.0 all-gather.18
  316.1 59.1 all-reduce.10
  377.2 42.1 all-gather.20
  425.4 59.0 all-reduce.12
  486.6 42.1 all-gather.22
  533.3 42.5 all-gather.24
  584.8 59.0 all-reduce.14
  645.9 42.1 all-gather.26
  693.3 59.1 all-reduce.16
  754.5 46.0 all-gather.28
  809.9 59.6 all-reduce.18
  871.7 55.9 all-gather.30
